TPU v7x, 128 devices: a whole 4x4x4 slice. The times are simulated.
128 devices in a mesh: px: 8 (over y, core), py: 16 (over x, z).
Axes of the slice: x: 4, y: 4, z: 4, core: 2. Of those that a mesh axis runs over, the one named last changes fastest.
Arguments:
- control_start: float32 [2, 16, 128, 2048], P(None, 'py', None, 'px'), may hold values from -12 to 12
- coef_x: float32 [16, 128, 2048], P('py', None, 'px'), may hold values from 0.1 to 0.45
- coef_y: float32 [16, 128, 2048], P('py', 'px'), may hold values from 0.1 to 0.45
- innovation: float32 [131072, 128], P(('px', 'py')), may hold values from -6 to 6
- obs_weight: float32 [131072, 128], P(('px', 'py')), may hold values from 0.25 to 4
- interp: float32 [131072], P(('px', 'py')), may hold values from 0 to 1
- obs_owner: int32 [131072, 1], P(('px', 'py')), may hold values from 0 to 15; in each aligned block of 1024 rows (0 to 1023, 1024 to 2047, ...) at most 192 rows name the same one
- cell_key: int32 [131072], P(('px', 'py')), may hold values from 0 to 31
- stencil: int32 [131072], P(('px', 'py')), may hold values from 0 to 14
Outputs:
- control: float32 [2, 16, 128, 2048], P(None, 'py', None, 'px')
- residual: float32 [2, 16, 128, 2048], P(None, 'py', None, 'px')
Inputs may be any that keep to these rules, and one draw needn't show every extreme that they name: `obs_owner`: at most 192 of the observation rows of one device name the same owner, and exactly 192 do for some owner on some device.
All inputs are finite; a program needn't handle non-finite values.
Results may differ from a plain program's by a relative error of at most 0.00023.
Values sent between devices are 32-bit elements; how exact they have to be, the bound alone decides.
A program may use at most 64 MiB of HBM per device.

v0:
```python
import jax
import jax.numpy as jnp
from jax import lax
from jax.sharding import PartitionSpec as P

F = 2
SEG = 128
M = 4
ITERS = 2
LZ = 1
LX = 16
NB = 16


def diffuse(values, coeffs, axis_dim):
    length = values.shape[axis_dim]
    face_coef = lax.slice_in_dim(coeffs[None], 0, length - 1, axis=axis_dim)
    pad_after = [(0, 0)] * values.ndim
    pad_before = [(0, 0)] * values.ndim
    pad_after[axis_dim] = (0, 1)
    pad_before[axis_dim] = (1, 0)
    for repeat in range(M):
        next_cell = lax.slice_in_dim(values, 1, length, axis=axis_dim)
        this_cell = lax.slice_in_dim(values, 0, length - 1, axis=axis_dim)
        flux_face = face_coef * (next_cell - this_cell)
        values = values + jnp.pad(flux_face, pad_after) - jnp.pad(flux_face, pad_before)
    return values


def build_interp(shares_in, rows_in, row_count):
    row_ids = jnp.arange(row_count, dtype=jnp.int32)[None, :]
    lower_hit = (rows_in[:, None] == row_ids).astype(jnp.float32)
    upper_hit = (rows_in[:, None] + NB == row_ids).astype(jnp.float32)
    shares = shares_in[:, None]
    return (1.0 - shares) * lower_hit + shares * upper_hit


def misfit(state_in, observed, weights, interp_matrix):
    flat_field = state_in.reshape(-1, SEG)
    modelled = jnp.dot(
        interp_matrix,
        flat_field,
        precision=lax.Precision.HIGHEST,
        preferred_element_type=jnp.float32,
    )
    weighted = weights * (observed - modelled)
    result = lax.dot_general(
        interp_matrix,
        weighted,
        (((0,), (0,)), ((), ())),
        precision=lax.Precision.HIGHEST,
        preferred_element_type=jnp.float32,
    )
    return result.reshape(state_in.shape)


def dot_total(left_side, right_side):
    return lax.psum(jnp.sum(left_side * right_side), ("px", "py"))


def shards(
    control_start, coef_x, coef_y, innovation, obs_weight, interp, obs_owner, cell_key, stencil
):
    groups = lax.axis_size("py")
    capacity = 3 * innovation.shape[0] // groups
    coef_x = coef_x.at[:, -1, :].set(0.0)
    coef_y = coef_y.at[:, :, -1].set(0.0)
    field_id = cell_key // (LZ * NB)
    level_local = cell_key // NB % LZ
    row_index = ((field_id * LZ + level_local) * LX + stencil) * NB + cell_key % NB
    targets = obs_owner[:, 0]
    onehot = (targets[:, None] == jnp.arange(groups, dtype=jnp.int32)[None, :]).astype(jnp.int32)
    earlier = jnp.cumsum(onehot, axis=0) - onehot
    slot_index = jnp.sum(earlier * onehot, axis=1)
    slot_target = targets * capacity + slot_index
    total_slots = groups * capacity

    def bucket(values_in):
        buf_shape = (total_slots,) + values_in.shape[1:]
        return jnp.zeros(buf_shape, values_in.dtype).at[slot_target].set(values_in)

    arrived = (
        lax.all_to_all(bucket(innovation), "py", split_axis=0, concat_axis=0, tiled=True),
        lax.all_to_all(bucket(obs_weight), "py", split_axis=0, concat_axis=0, tiled=True),
        lax.all_to_all(bucket(interp), "py", split_axis=0, concat_axis=0, tiled=True),
        lax.all_to_all(bucket(row_index), "py", split_axis=0, concat_axis=0, tiled=True),
    )
    observed, weights, shares_in, rows_in = arrived
    interp_matrix = build_interp(shares_in, rows_in, F * LZ * LX * NB)

    def forward(values_in):
        turned = lax.all_to_all(
            diffuse(values_in, coef_x, 2), "px", split_axis=2, concat_axis=3, tiled=True
        )
        return diffuse(turned, coef_y, 3)

    def adjoint(values_in):
        turned = lax.all_to_all(
            diffuse(values_in, coef_y, 3), "px", split_axis=3, concat_axis=2, tiled=True
        )
        return diffuse(turned, coef_x, 2)

    no_data = jnp.zeros_like(observed)
    residual = (
        adjoint(misfit(forward(control_start), observed, weights, interp_matrix)) - control_start
    )
    control = control_start
    direction = residual
    norm_now = dot_total(residual, residual)
    for repeat in range(ITERS):
        applied = direction - adjoint(misfit(forward(direction), no_data, weights, interp_matrix))
        step_size = norm_now / dot_total(direction, applied)
        control = control + step_size * direction
        residual = residual - step_size * applied
        norm_next = dot_total(residual, residual)
        direction = residual + norm_next / norm_now * direction
        norm_now = norm_next
    return (control, residual)


def solution(mesh):
    return jax.shard_map(
        shards,
        mesh=mesh,
        in_specs=(
            P(None, "py", None, "px"),
            P("py", None, "px"),
            P("py", "px", None),
            P(("px", "py"), None),
            P(("px", "py"), None),
            P(("px", "py")),
            P(("px", "py"), None),
            P(("px", "py")),
            P(("px", "py")),
        ),
        out_specs=(P(None, "py", None, "px"), P(None, "py", None, "px")),
        check_vma=False,
    )
```

profile of v0, /device:TPU:1, one launch (start us, length us, event | category | flops | bytes accessed | tf_op | source)
XLA Modules:
  0.0 462.8 jit_solution(5884328285071608332)
XLA Ops:
  1.4 4.5 reduce-window.6
  8.4 4.3 scatter_custom_fusion
  13.5 8.4 %all-to-all-start = ((s32[16,192,1]{1,2,0:T(1,128)}), s32[16,192,1]{1,2,0:T(1,128)S(1)}, u32[]{:S(2)}, u32[]{:S(2)}) async-start(s32[16,192,1]{1,2,0:T(1,128)} %all_to_all.143), calls=%async_computation | async-start | bytes 32768 | tf_op jit(solution)/shard_map/all_to_all | solution.py:86
  24.9 4.5 scatter_custom_fusion.1
  30.0 6.7 %all-to-all-start.1 = ((f32[16,192,1]{1,2,0:T(1,128)}), f32[16,192,1]{1,2,0:T(1,128)S(1)}, u32[]{:S(2)}, u32[]{:S(2)}) async-start(f32[16,192,1]{1,2,0:T(1,128)} %all_to_all.144), calls=%async_computation.1 | async-start | bytes 32768 | tf_op jit(solution)/shard_map/all_to_all | solution.py:85
  36.8 4.7 %scatter_custom_fusion.2 = f32[3072,128]{1,0:T(8,128)} fusion(s32[1024]{0:T(1024)S(1)} %bitcast.132, f32[1024,128]{1,0:T(8,128)} %param.17, f32[]{:T(128)} %constant.119.clone.1), kind=kCustom, calls=%fused_computation.51 | custom fusion | bytes 1573376 | tf_op jit(solution)/shard_map/scatter | solution.py:80
  41.5 4.7 %scatter_custom_fusion.3 = f32[3072,128]{1,0:T(8,128)} fusion(s32[1024]{0:T(1024)S(1)} %bitcast.133, f32[1024,128]{1,0:T(8,128)} %param.16, f32[]{:T(128)} %constant.119.clone.1), kind=kCustom, calls=%fused_computation.49 | custom fusion | bytes 1573376 | tf_op jit(solution)/shard_map/scatter | solution.py:80
  47.2 6.0 %all-to-all-start.4 = ((f32[2,1,128,256]{3,0,1,2:T(2,128)}), f32[2,1,128,256]{3,0,1,2:T(2,128)S(1)}, u32[]{:S(2)}, u32[]{:S(2)}) async-start(f32[2,1,128,256]{3,0,1,2:T(2,128)} %copy.120), calls=%async_computation.4 | async-start | bytes 524288 | tf_op jit(solution)/shard_map/all_to_all | solution.py:92
  53.3 6.4 %all-to-all-done.4 = f32[2,1,128,256]{3,0,1,2:T(2,128)S(1)} async-done(((f32[2,1,128,256]{3,0,1,2:T(2,128)}), f32[2,1,128,256]{3,0,1,2:T(2,128)S(1)}, u32[]{:S(2)}, u32[]{:S(2)}) %all-to-all-start.4) | async-done | bytes 262176 | tf_op jit(solution)/shard_map/all_to_all | solution.py:92
  59.6 6.9 %all-to-all-start.2 = ((f32[16,192,128]{2,1,0:T(8,128)}), f32[16,192,128]{2,1,0:T(8,128)S(1)}, u32[]{:S(2)}, u32[]{:S(2)}) async-start(f32[16,192,128]{2,1,0:T(8,128)} %bitcast.7), calls=%async_computation.2 | async-start | bytes 3145728 | tf_op jit(solution)/shard_map/all_to_all | solution.py:84
  67.2 19.9 %all-to-all-done.2 = f32[16,192,128]{2,1,0:T(8,128)S(1)} async-done(((f32[16,192,128]{2,1,0:T(8,128)}), f32[16,192,128]{2,1,0:T(8,128)S(1)}, u32[]{:S(2)}, u32[]{:S(2)}) %all-to-all-start.2) | async-done | bytes 1572896 | tf_op jit(solution)/shard_map/all_to_all | solution.py:84
  87.1 4.7 %all-to-all-start.3 = ((f32[16,192,128]{2,1,0:T(8,128)}), f32[16,192,128]{2,1,0:T(8,128)}, u32[]{:S(2)}, u32[]{:S(2)}) async-start(f32[16,192,128]{2,1,0:T(8,128)} %bitcast.9), calls=%async_computation.3 | async-start | bytes 3145728 | tf_op jit(solution)/shard_map/all_to_all | solution.py:83
  92.4 18.5 %all-to-all-done.3 = f32[16,192,128]{2,1,0:T(8,128)} async-done(((f32[16,192,128]{2,1,0:T(8,128)}), f32[16,192,128]{2,1,0:T(8,128)}, u32[]{:S(2)}, u32[]{:S(2)}) %all-to-all-start.3) | async-done | bytes 1572896 | tf_op jit(solution)/shard_map/all_to_all | solution.py:83
  111.0 9.5 %fusion.11 = f32[3072,128]{1,0:T(8,128)S(1)} fusion(f32[3072,128]{1,0:T(8,128)S(1)} %bitcast.117, f32[3072,128]{1,0:T(8,128)} %bitcast.10, f32[512,128]{1,0:T(8,128)S(1)} %reshape.123, f32[3072]{0:T(1024)S(1)} %all_to_all.112, s32[3072]{0:T(1024)S(1)} %broadcast_add_fusion.1, f32[3072]{0:T(1024)S(1)} %broadcast_subtract_fusion, s32[3072]{0:T(1024)S(1)} %eq.64), kind=kOutput, calls=%fused_computation.18 | convolution fusion | flops 2424569856 | bytes 5029888 | tf_op jit(solution)/shard_map/dot_general | solution.py:40
  120.5 11.8 %fusion.4 = f32[512,128]{1,0:T(8,128)S(1)} fusion(f32[3072,128]{1,0:T(8,128)S(1)} %fusion.11, f32[3072]{0:T(1024)S(1)} %all_to_all.112, s32[3072]{0:T(1024)S(1)} %broadcast_add_fusion.1, f32[3072]{0:T(1024)S(1)} %broadcast_subtract_fusion, s32[3072]{0:T(1024)S(1)} %eq.64), kind=kOutput, calls=%fused_computation.10 | convolution fusion | flops 2423783424 | bytes 1884160 | tf_op jit(solution)/shard_map/dot_general | solution.py:47
  134.7 2.9 reshape.171
  137.6 14.4 %all_to_all.155 = f32[8,1,8192]{2,1,0:T(1,128)S(1)} all-to-all(f32[8,1,8192]{2,1,0:T(1,128)S(1)} %reshape.171), channel_id=1, replica_groups=mesh['px'=8,'py'=16] {'px'}, dimensions={0} | all-to-all | bytes 524288 | tf_op jit(solution)/shard_map/all_to_all | solution.py:98
  158.4 9.9 %all_to_all.156 = f32[2,1,128,256]{3,0,1,2:T(2,128)S(1)} all-to-all(f32[2,1,128,256]{3,0,1,2:T(2,128)S(1)} %copy.127), channel_id=1, replica_groups=mesh['px'=8,'py'=16] {'px'}, dimensions={2} | all-to-all | bytes 524288 | tf_op jit(solution)/shard_map/all_to_all | solution.py:92
  170.3 9.1 %fusion.10 = f32[3072,128]{1,0:T(8,128)S(1)} fusion(f32[3072,128]{1,0:T(8,128)S(1)} %bitcast.118, f32[512,128]{1,0:T(8,128)S(1)} %reshape.125, f32[3072]{0:T(1024)S(1)} %all_to_all.112, s32[3072]{0:T(1024)S(1)} %broadcast_add_fusion.1, f32[3072]{0:T(1024)S(1)} %broadcast_subtract_fusion, s32[3072]{0:T(1024)S(1)} %eq.64), kind=kOutput, calls=%fused_computation.17 | convolution fusion | flops 2424569856 | bytes 3457024 | tf_op jit(solution)/shard_map/dot_general | solution.py:40
  179.5 11.8 %fusion.2 = f32[512,128]{1,0:T(8,128)S(1)} fusion(f32[3072,128]{1,0:T(8,128)S(1)} %fusion.10, f32[3072]{0:T(1024)S(1)} %all_to_all.112, s32[3072]{0:T(1024)S(1)} %broadcast_add_fusion.1, f32[3072]{0:T(1024)S(1)} %broadcast_subtract_fusion, s32[3072]{0:T(1024)S(1)} %eq.64), kind=kOutput, calls=%fused_computation.8 | convolution fusion | flops 2423783424 | bytes 1884160 | tf_op jit(solution)/shard_map/dot_general | solution.py:47
  193.9 2.9 reshape.173
  196.8 9.9 %all_to_all.157 = f32[8,1,8192]{2,1,0:T(1,128)S(1)} all-to-all(f32[8,1,8192]{2,1,0:T(1,128)S(1)} %reshape.173), channel_id=1, replica_groups=mesh['px'=8,'py'=16] {'px'}, dimensions={0} | all-to-all | bytes 524288 | tf_op jit(solution)/shard_map/all_to_all | solution.py:98
  208.0 2.8 reshape.174
  212.7 63.0 %all-reduce.96 = (f32[]{:T(128)}, f32[]{:T(128)}) all-reduce(f32[]{:T(128)} %get-tuple-element.35, f32[]{:T(128)} %get-tuple-element.34), channel_id=1, replica_groups=mesh['px'=8,'py'=16] {'px','py'}, use_global_device_ids=true, to_apply=%region_8.9 | all-reduce | flops 2 | bytes 16 | tf_op jit(solution)/shard_map/psum | solution.py:58
  277.7 62.5 %psum.30 = f32[]{:T(128)} all-reduce(f32[]{:T(128)} %get-tuple-element.38), channel_id=1, replica_groups=mesh['px'=8,'py'=16] {'px','py'}, use_global_device_ids=true, to_apply=%region_12.13 | all-reduce | flops 1 | bytes 8 | tf_op jit(solution)/shard_map/psum | solution.py:58
  342.1 11.0 %all_to_all.158 = f32[2,1,128,256]{3,0,1,2:T(2,128)S(1)} all-to-all(f32[2,1,128,256]{3,0,1,2:T(2,128)S(1)} %copy.134), channel_id=1, replica_groups=mesh['px'=8,'py'=16] {'px'}, dimensions={2} | all-to-all | bytes 524288 | tf_op jit(solution)/shard_map/all_to_all | solution.py:92
  355.1 9.1 %fusion.9 = f32[3072,128]{1,0:T(8,128)S(1)} fusion(f32[3072,128]{1,0:T(8,128)S(1)} %bitcast.119, f32[512,128]{1,0:T(8,128)S(1)} %reshape.127, f32[3072]{0:T(1024)S(1)} %all_to_all.112, s32[3072]{0:T(1024)S(1)} %broadcast_add_fusion.1, f32[3072]{0:T(1024)S(1)} %broadcast_subtract_fusion, s32[3072]{0:T(1024)S(1)} %eq.64), kind=kOutput, calls=%fused_computation.16 | convolution fusion | flops 2424569856 | bytes 3457024 | tf_op jit(solution)/shard_map/dot_general | solution.py:40
  364.2 11.8 %fusion = f32[512,128]{1,0:T(8,128)S(1)} fusion(f32[3072,128]{1,0:T(8,128)S(1)} %fusion.9, f32[3072]{0:T(1024)S(1)} %all_to_all.112, s32[3072]{0:T(1024)S(1)} %broadcast_add_fusion.1, f32[3072]{0:T(1024)S(1)} %broadcast_subtract_fusion, s32[3072]{0:T(1024)S(1)} %eq.64), kind=kOutput, calls=%fused_computation.6 | convolution fusion | flops 2423783424 | bytes 1884160 | tf_op jit(solution)/shard_map/dot_general | solution.py:47
  378.4 2.9 reshape.175
  381.3 9.9 %all_to_all.159 = f32[8,1,8192]{2,1,0:T(1,128)S(1)} all-to-all(f32[8,1,8192]{2,1,0:T(1,128)S(1)} %reshape.175), channel_id=1, replica_groups=mesh['px'=8,'py'=16] {'px'}, dimensions={0} | all-to-all | bytes 524288 | tf_op jit(solution)/shard_map/all_to_all | solution.py:98
  392.5 2.8 reshape.176
  397.2 63.1 %psum.31 = f32[]{:T(128)} all-reduce(f32[]{:T(128)} %multiply_reduce_fusion), channel_id=1, replica_groups=mesh['px'=8,'py'=16] {'px','py'}, use_global_device_ids=true, to_apply=%region_14.15 | all-reduce | flops 1 | bytes 8 | tf_op jit(solution)/shard_map/psum | solution.py:58
  (161 shorter events, 35.6 us)
Async XLA Ops:
  0.6 23.3 %copy-start = (f32[2,1,128,256]{3,2,1,0:T(8,128)S(1)}, f32[2,1,128,256]{3,2,1,0:T(8,128)}, u32[]{:S(2)}) copy-start(f32[2,1,128,256]{3,2,1,0:T(8,128)} %param.13) | copy-start | bytes 786436
  13.5 16.6 %all-to-all-start = ((s32[16,192,1]{1,2,0:T(1,128)}), s32[16,192,1]{1,2,0:T(1,128)S(1)}, u32[]{:S(2)}, u32[]{:S(2)}) async-start(s32[16,192,1]{1,2,0:T(1,128)} %all_to_all.143), calls=%async_computation | async-start | bytes 32768 | tf_op jit(solution)/shard_map/all_to_all | solution.py:86
  23.9 0.9 copy-start.6
  30.0 17.1 %all-to-all-start.1 = ((f32[16,192,1]{1,2,0:T(1,128)}), f32[16,192,1]{1,2,0:T(1,128)S(1)}, u32[]{:S(2)}, u32[]{:S(2)}) async-start(f32[16,192,1]{1,2,0:T(1,128)} %all_to_all.144), calls=%async_computation.1 | async-start | bytes 32768 | tf_op jit(solution)/shard_map/all_to_all | solution.py:85
  47.2 12.5 %all-to-all-start.4 = ((f32[2,1,128,256]{3,0,1,2:T(2,128)}), f32[2,1,128,256]{3,0,1,2:T(2,128)S(1)}, u32[]{:S(2)}, u32[]{:S(2)}) async-start(f32[2,1,128,256]{3,0,1,2:T(2,128)} %copy.120), calls=%async_computation.4 | async-start | bytes 524288 | tf_op jit(solution)/shard_map/all_to_all | solution.py:92
  59.6 27.5 %all-to-all-start.2 = ((f32[16,192,128]{2,1,0:T(8,128)}), f32[16,192,128]{2,1,0:T(8,128)S(1)}, u32[]{:S(2)}, u32[]{:S(2)}) async-start(f32[16,192,128]{2,1,0:T(8,128)} %bitcast.7), calls=%async_computation.2 | async-start | bytes 3145728 | tf_op jit(solution)/shard_map/all_to_all | solution.py:84
  87.1 23.8 %copy-start.3 = (f32[16,192,128]{2,1,0:T(8,128)}, f32[16,192,128]{2,1,0:T(8,128)S(1)}, u32[]{:S(2)}) copy-start(f32[16,192,128]{2,1,0:T(8,128)S(1)} %all-to-all-done.2) | copy-start | bytes 4718596
  87.1 23.8 %all-to-all-start.3 = ((f32[16,192,128]{2,1,0:T(8,128)}), f32[16,192,128]{2,1,0:T(8,128)}, u32[]{:S(2)}, u32[]{:S(2)}) async-start(f32[16,192,128]{2,1,0:T(8,128)} %bitcast.9), calls=%async_computation.3 | async-start | bytes 3145728 | tf_op jit(solution)/shard_map/all_to_all | solution.py:83
  168.9 1.4 copy-start.4
  277.7 63.8 %copy-start.1 = (f32[2,1,128,256]{3,2,0,1:T(8,128)}, f32[2,1,128,256]{3,2,0,1:T(8,128)S(1)}, u32[]{:S(2)}) copy-start(f32[2,1,128,256]{3,2,0,1:T(8,128)S(1)} %get-tuple-element.39) | copy-start | bytes 786436
  353.7 1.4 copy-start.5
  396.3 65.3 %copy-start.2 = (f32[2,1,128,256]{3,2,0,1:T(8,128)S(1)}, f32[2,1,128,256]{3,2,0,1:T(8,128)}, u32[]{:S(2)}) copy-start(f32[2,1,128,256]{3,2,0,1:T(8,128)} %copy-done.1) | copy-start | bytes 786436
where the time goes:
time: 471 us; the launch traced here: 463 us
  blocking collectives  244 us (52%)
  matrix products  63.2 us (13%)
  local copies, waits for them, and re-layouts  47.9 us (10%)
  waiting for transfers between devices  44.8 us (10%)
  starting transfers between devices  32.7 us (7%)
  other arithmetic  24.5 us (5%)
  between operations  5.82 us (1%)
    psum x3, blocking collectives, dot_total(): return lax.psum(jnp.sum(left_side * right_side), ('px', 'py'))  189 us
    dot_general x3, matrix products, misfit(): lax.dot_general(interp_matrix, weighted, (((0,), (0,)), ((), ())), precis...  35.4 us
    all_to_all x3, blocking collectives, adjoint(): lax.all_to_all(diffuse(values_in, coef_y, 3), 'px', split_axis=3, concat_...  34.3 us
    dot_general x3, matrix products, misfit(): jnp.dot(interp_matrix, flat_field, precision=lax.Precision.HIGHEST, prefe...  27.7 us
    all_to_all x2, blocking collectives, forward(): lax.all_to_all(diffuse(values_in, coef_x, 2), 'px', split_axis=2, concat_...  20.9 us
    all_to_all x1, waiting for transfers between devices, shards(): lax.all_to_all(bucket(obs_weight), 'py', split_axis=0, concat_axis=0, til...  19.9 us
    unnamed x20, local copies, waits for them, and re-layouts  19.2 us
    all_to_all x1, waiting for transfers between devices, shards(): lax.all_to_all(bucket(innovation), 'py', split_axis=0, concat_axis=0, til...  18.5 us
  transfers between devices with their start and end apart: 5, of which 3 were waited for; matrix products, arithmetic and copies ran while one was open for 4% of the time, Pallas kernels for 0%

commit v1 on v0

--- a/solution.py
+++ b/solution.py
@@ -89,8 +89,14 @@
     interp_matrix = build_interp(shares_in, rows_in, F * LZ * LX * NB)
 
     def forward(values_in):
-        turned = lax.all_to_all(
-            diffuse(values_in, coef_x, 2), "px", split_axis=2, concat_axis=3, tiled=True
+        turned = jnp.concatenate(
+            lax.all_to_all(
+                jnp.stack(jnp.split(diffuse(values_in, coef_x, 2), lax.axis_size("px"), axis=2)),
+                "px",
+                0,
+                0,
+            ),
+            axis=3,
         )
         return diffuse(turned, coef_y, 3)
 

time: 471 us -> 474 us (level)
    unnamed x20 -> x41, local copies, waits for them, and re-layouts: 19.2 us -> 23 us
  transfers between devices with their start and end apart: 5 -> 5, of which waited for: 3 -> 3; matrix products, arithmetic and copies ran while one was open for 4% -> 5% of each run, Pallas kernels for 0% -> 0%
where the time goes in v1:
time: 474 us; the launch traced here: 466 us
  blocking collectives  244 us (51%)
  matrix products  63.1 us (13%)
  local copies, waits for them, and re-layouts  50.9 us (11%)
  waiting for transfers between devices  44.9 us (9%)
  starting transfers between devices  32.7 us (7%)
  other arithmetic  24.5 us (5%)
  between operations  5.92 us (1%)
    psum x3, blocking collectives, dot_total(): return lax.psum(jnp.sum(left_side * right_side), ('px', 'py'))  189 us
    dot_general x3, matrix products, misfit(): lax.dot_general(interp_matrix, weighted, (((0,), (0,)), ((), ())), precis...  35.4 us
    all_to_all x3, blocking collectives, adjoint(): lax.all_to_all(diffuse(values_in, coef_y, 3), 'px', split_axis=3, concat_...  34.3 us
    dot_general x3, matrix products, misfit(): jnp.dot(interp_matrix, flat_field, precision=lax.Precision.HIGHEST, prefe...  27.7 us
    unnamed x41, local copies, waits for them, and re-layouts  23 us
    all_to_all x2, blocking collectives, forward(): lax.all_to_all(jnp.stack(jnp.split(diffuse(values_in, coef_x, 2), lax.axi...  20.9 us
    all_to_all x1, waiting for transfers between devices, shards(): lax.all_to_all(bucket(obs_weight), 'py', split_axis=0, concat_axis=0, til...  19.9 us
    all_to_all x1, waiting for transfers between devices, shards(): lax.all_to_all(bucket(innovation), 'py', split_axis=0, concat_axis=0, til...  18.5 us
  transfers between devices with their start and end apart: 5, of which 3 were waited for; matrix products, arithmetic and copies ran while one was open for 5% of the time, Pallas kernels for 0%

profile of v1, /device:TPU:1, one launch (start us, length us, event | category | flops | bytes accessed | tf_op | source)
XLA Modules:
  0.0 465.9 jit_solution(7660563149025196484)
XLA Ops:
  1.4 4.5 reduce-window.6
  8.4 4.3 scatter_custom_fusion
  13.4 8.4 %all-to-all-start = ((s32[16,192,1]{1,2,0:T(1,128)}), s32[16,192,1]{1,2,0:T(1,128)S(1)}, u32[]{:S(2)}, u32[]{:S(2)}) async-start(s32[16,192,1]{1,2,0:T(1,128)} %all_to_all.104), calls=%async_computation | async-start | bytes 32768 | tf_op jit(solution)/shard_map/all_to_all | solution.py:86
  28.6 4.5 scatter_custom_fusion.1
  33.8 6.7 %all-to-all-start.1 = ((f32[16,192,1]{1,2,0:T(1,128)}), f32[16,192,1]{1,2,0:T(1,128)S(1)}, u32[]{:S(2)}, u32[]{:S(2)}) async-start(f32[16,192,1]{1,2,0:T(1,128)} %all_to_all.105), calls=%async_computation.1 | async-start | bytes 32768 | tf_op jit(solution)/shard_map/all_to_all | solution.py:85
  41.0 4.7 %scatter_custom_fusion.2 = f32[3072,128]{1,0:T(8,128)} fusion(s32[1024]{0:T(1024)S(1)} %bitcast.248, f32[1024,128]{1,0:T(8,128)} %param.17, f32[]{:T(128)} %constant.119.clone.1), kind=kCustom, calls=%fused_computation.51 | custom fusion | bytes 1573376 | tf_op jit(solution)/shard_map/scatter | solution.py:80
  45.7 4.7 %scatter_custom_fusion.3 = f32[3072,128]{1,0:T(8,128)} fusion(s32[1024]{0:T(1024)S(1)} %bitcast.249, f32[1024,128]{1,0:T(8,128)} %param.16, f32[]{:T(128)} %constant.119.clone.1), kind=kCustom, calls=%fused_computation.49 | custom fusion | bytes 1573376 | tf_op jit(solution)/shard_map/scatter | solution.py:80
  50.5 6.0 %all-to-all-start.4 = ((f32[8,2,1,16,256]{4,3,1,2,0:T(8,128)}), f32[8,2,1,16,256]{4,3,1,2,0:T(8,128)S(1)}, u32[]{:S(2)}, u32[]{:S(2)}) async-start(f32[8,2,1,16,256]{4,3,1,2,0:T(8,128)} %constant_dynamic-update-slice_fusion), calls=%async_computation.4 | async-start | bytes 524288 | tf_op jit(solution)/shard_map/all_to_all | solution.py:93
  56.6 6.4 %all-to-all-done.4 = f32[8,2,1,16,256]{4,3,1,2,0:T(8,128)S(1)} async-done(((f32[8,2,1,16,256]{4,3,1,2,0:T(8,128)}), f32[8,2,1,16,256]{4,3,1,2,0:T(8,128)S(1)}, u32[]{:S(2)}, u32[]{:S(2)}) %all-to-all-start.4) | async-done | bytes 262176 | tf_op jit(solution)/shard_map/all_to_all | solution.py:93
  63.0 6.9 %all-to-all-start.2 = ((f32[16,192,128]{2,1,0:T(8,128)}), f32[16,192,128]{2,1,0:T(8,128)S(1)}, u32[]{:S(2)}, u32[]{:S(2)}) async-start(f32[16,192,128]{2,1,0:T(8,128)} %bitcast.6), calls=%async_computation.2 | async-start | bytes 3145728 | tf_op jit(solution)/shard_map/all_to_all | solution.py:84
  70.5 19.9 %all-to-all-done.2 = f32[16,192,128]{2,1,0:T(8,128)S(1)} async-done(((f32[16,192,128]{2,1,0:T(8,128)}), f32[16,192,128]{2,1,0:T(8,128)S(1)}, u32[]{:S(2)}, u32[]{:S(2)}) %all-to-all-start.2) | async-done | bytes 1572896 | tf_op jit(solution)/shard_map/all_to_all | solution.py:84
  90.5 4.7 %all-to-all-start.3 = ((f32[16,192,128]{2,1,0:T(8,128)}), f32[16,192,128]{2,1,0:T(8,128)}, u32[]{:S(2)}, u32[]{:S(2)}) async-start(f32[16,192,128]{2,1,0:T(8,128)} %bitcast.8), calls=%async_computation.3 | async-start | bytes 3145728 | tf_op jit(solution)/shard_map/all_to_all | solution.py:83
  95.8 18.5 %all-to-all-done.3 = f32[16,192,128]{2,1,0:T(8,128)} async-done(((f32[16,192,128]{2,1,0:T(8,128)}), f32[16,192,128]{2,1,0:T(8,128)}, u32[]{:S(2)}, u32[]{:S(2)}) %all-to-all-start.3) | async-done | bytes 1572896 | tf_op jit(solution)/shard_map/all_to_all | solution.py:83
  114.3 9.5 %fusion.11 = f32[3072,128]{1,0:T(8,128)S(1)} fusion(f32[3072,128]{1,0:T(8,128)S(1)} %bitcast.212, f32[3072,128]{1,0:T(8,128)} %bitcast.9, f32[512,128]{1,0:T(8,128)S(1)} %reshape.143, f32[3072]{0:T(1024)S(1)} %all_to_all.82, s32[3072]{0:T(1024)S(1)} %broadcast_add_fusion.1, f32[3072]{0:T(1024)S(1)} %broadcast_subtract_fusion, s32[3072]{0:T(1024)S(1)} %eq.64), kind=kOutput, calls=%fused_computation.18 | convolution fusion | flops 2424569856 | bytes 5029888 | tf_op jit(solution)/shard_map/dot_general | solution.py:40
  123.9 11.8 %fusion.4 = f32[512,128]{1,0:T(8,128)S(1)} fusion(f32[3072,128]{1,0:T(8,128)S(1)} %fusion.11, f32[3072]{0:T(1024)S(1)} %all_to_all.82, s32[3072]{0:T(1024)S(1)} %broadcast_add_fusion.1, f32[3072]{0:T(1024)S(1)} %broadcast_subtract_fusion, s32[3072]{0:T(1024)S(1)} %eq.64), kind=kOutput, calls=%fused_computation.10 | convolution fusion | flops 2423783424 | bytes 1884160 | tf_op jit(solution)/shard_map/dot_general | solution.py:47
  138.1 2.9 reshape.195
  140.9 14.4 %all_to_all.116 = f32[8,1,8192]{2,1,0:T(1,128)S(1)} all-to-all(f32[8,1,8192]{2,1,0:T(1,128)S(1)} %reshape.195), channel_id=1, replica_groups=mesh['px'=8,'py'=16] {'px'}, dimensions={0} | all-to-all | bytes 524288 | tf_op jit(solution)/shard_map/all_to_all | solution.py:104
  157.1 2.8 reshape.196
  161.6 9.9 %all_to_all.117 = f32[8,2,1,16,256]{4,3,1,2,0:T(8,128)S(1)} all-to-all(f32[8,2,1,16,256]{4,3,1,2,0:T(8,128)S(1)} %constant_dynamic-update-slice_fusion.8), channel_id=1, replica_groups=mesh['px'=8,'py'=16] {'px'}, dimensions={0} | all-to-all | bytes 524288 | tf_op jit(solution)/shard_map/all_to_all | solution.py:93
  173.6 9.1 %fusion.10 = f32[3072,128]{1,0:T(8,128)S(1)} fusion(f32[3072,128]{1,0:T(8,128)S(1)} %bitcast.213, f32[512,128]{1,0:T(8,128)S(1)} %reshape.147, f32[3072]{0:T(1024)S(1)} %all_to_all.82, s32[3072]{0:T(1024)S(1)} %broadcast_add_fusion.1, f32[3072]{0:T(1024)S(1)} %broadcast_subtract_fusion, s32[3072]{0:T(1024)S(1)} %eq.64), kind=kOutput, calls=%fused_computation.17 | convolution fusion | flops 2424569856 | bytes 3457024 | tf_op jit(solution)/shard_map/dot_general | solution.py:40
  182.7 11.8 %fusion.2 = f32[512,128]{1,0:T(8,128)S(1)} fusion(f32[3072,128]{1,0:T(8,128)S(1)} %fusion.10, f32[3072]{0:T(1024)S(1)} %all_to_all.82, s32[3072]{0:T(1024)S(1)} %broadcast_add_fusion.1, f32[3072]{0:T(1024)S(1)} %broadcast_subtract_fusion, s32[3072]{0:T(1024)S(1)} %eq.64), kind=kOutput, calls=%fused_computation.8 | convolution fusion | flops 2423783424 | bytes 1884160 | tf_op jit(solution)/shard_map/dot_general | solution.py:47
  197.1 2.9 reshape.197
  200.0 9.9 %all_to_all.118 = f32[8,1,8192]{2,1,0:T(1,128)S(1)} all-to-all(f32[8,1,8192]{2,1,0:T(1,128)S(1)} %reshape.197), channel_id=1, replica_groups=mesh['px'=8,'py'=16] {'px'}, dimensions={0} | all-to-all | bytes 524288 | tf_op jit(solution)/shard_map/all_to_all | solution.py:104
  211.2 2.8 reshape.198
  216.0 63.0 %all-reduce.96 = (f32[]{:T(128)}, f32[]{:T(128)}) all-reduce(f32[]{:T(128)} %get-tuple-element.27, f32[]{:T(128)} %get-tuple-element.26), channel_id=1, replica_groups=mesh['px'=8,'py'=16] {'px','py'}, use_global_device_ids=true, to_apply=%region_8.9 | all-reduce | flops 2 | bytes 16 | tf_op jit(solution)/shard_map/psum | solution.py:58
  281.0 62.5 %psum.30 = f32[]{:T(128)} all-reduce(f32[]{:T(128)} %get-tuple-element.30), channel_id=1, replica_groups=mesh['px'=8,'py'=16] {'px','py'}, use_global_device_ids=true, to_apply=%region_12.13 | all-reduce | flops 1 | bytes 8 | tf_op jit(solution)/shard_map/psum | solution.py:58
  345.3 11.0 %all_to_all.119 = f32[8,2,1,16,256]{4,3,1,2,0:T(8,128)S(1)} all-to-all(f32[8,2,1,16,256]{4,3,1,2,0:T(8,128)S(1)} %constant_dynamic-update-slice_fusion.16), channel_id=1, replica_groups=mesh['px'=8,'py'=16] {'px'}, dimensions={0} | all-to-all | bytes 524288 | tf_op jit(solution)/shard_map/all_to_all | solution.py:93
  358.2 9.1 %fusion.9 = f32[3072,128]{1,0:T(8,128)S(1)} fusion(f32[3072,128]{1,0:T(8,128)S(1)} %bitcast.214, f32[512,128]{1,0:T(8,128)S(1)} %reshape.151, f32[3072]{0:T(1024)S(1)} %all_to_all.82, s32[3072]{0:T(1024)S(1)} %broadcast_add_fusion.1, f32[3072]{0:T(1024)S(1)} %broadcast_subtract_fusion, s32[3072]{0:T(1024)S(1)} %eq.64), kind=kOutput, calls=%fused_computation.16 | convolution fusion | flops 2424569856 | bytes 3457024 | tf_op jit(solution)/shard_map/dot_general | solution.py:40
  367.3 11.8 %fusion = f32[512,128]{1,0:T(8,128)S(1)} fusion(f32[3072,128]{1,0:T(8,128)S(1)} %fusion.9, f32[3072]{0:T(1024)S(1)} %all_to_all.82, s32[3072]{0:T(1024)S(1)} %broadcast_add_fusion.1, f32[3072]{0:T(1024)S(1)} %broadcast_subtract_fusion, s32[3072]{0:T(1024)S(1)} %eq.64), kind=kOutput, calls=%fused_computation.6 | convolution fusion | flops 2423783424 | bytes 1884160 | tf_op jit(solution)/shard_map/dot_general | solution.py:47
  381.5 2.9 reshape.199
  384.4 9.9 %all_to_all.120 = f32[8,1,8192]{2,1,0:T(1,128)S(1)} all-to-all(f32[8,1,8192]{2,1,0:T(1,128)S(1)} %reshape.199), channel_id=1, replica_groups=mesh['px'=8,'py'=16] {'px'}, dimensions={0} | all-to-all | bytes 524288 | tf_op jit(solution)/shard_map/all_to_all | solution.py:104
  400.3 63.1 %psum.31 = f32[]{:T(128)} all-reduce(f32[]{:T(128)} %multiply_reduce_fusion), channel_id=1, replica_groups=mesh['px'=8,'py'=16] {'px','py'}, use_global_device_ids=true, to_apply=%region_14.15 | all-reduce | flops 1 | bytes 8 | tf_op jit(solution)/shard_map/psum | solution.py:58
  (179 shorter events, 38.6 us)
Async XLA Ops:
  0.6 23.2 %copy-start = (f32[2,1,128,256]{3,2,1,0:T(8,128)S(1)}, f32[2,1,128,256]{3,2,1,0:T(8,128)}, u32[]{:S(2)}) copy-start(f32[2,1,128,256]{3,2,1,0:T(8,128)} %param.13) | copy-start | bytes 786436
  13.4 20.3 %all-to-all-start = ((s32[16,192,1]{1,2,0:T(1,128)}), s32[16,192,1]{1,2,0:T(1,128)S(1)}, u32[]{:S(2)}, u32[]{:S(2)}) async-start(s32[16,192,1]{1,2,0:T(1,128)} %all_to_all.104), calls=%async_computation | async-start | bytes 32768 | tf_op jit(solution)/shard_map/all_to_all | solution.py:86
  24.0 3.9 copy-start.6
  33.8 16.8 %all-to-all-start.1 = ((f32[16,192,1]{1,2,0:T(1,128)}), f32[16,192,1]{1,2,0:T(1,128)S(1)}, u32[]{:S(2)}, u32[]{:S(2)}) async-start(f32[16,192,1]{1,2,0:T(1,128)} %all_to_all.105), calls=%async_computation.1 | async-start | bytes 32768 | tf_op jit(solution)/shard_map/all_to_all | solution.py:85
  50.5 12.5 %all-to-all-start.4 = ((f32[8,2,1,16,256]{4,3,1,2,0:T(8,128)}), f32[8,2,1,16,256]{4,3,1,2,0:T(8,128)S(1)}, u32[]{:S(2)}, u32[]{:S(2)}) async-start(f32[8,2,1,16,256]{4,3,1,2,0:T(8,128)} %constant_dynamic-update-slice_fusion), calls=%async_computation.4 | async-start | bytes 524288 | tf_op jit(solution)/shard_map/all_to_all | solution.py:93
  63.0 27.5 %all-to-all-start.2 = ((f32[16,192,128]{2,1,0:T(8,128)}), f32[16,192,128]{2,1,0:T(8,128)S(1)}, u32[]{:S(2)}, u32[]{:S(2)}) async-start(f32[16,192,128]{2,1,0:T(8,128)} %bitcast.6), calls=%async_computation.2 | async-start | bytes 3145728 | tf_op jit(solution)/shard_map/all_to_all | solution.py:84
  90.5 23.8 %copy-start.3 = (f32[16,192,128]{2,1,0:T(8,128)}, f32[16,192,128]{2,1,0:T(8,128)S(1)}, u32[]{:S(2)}) copy-start(f32[16,192,128]{2,1,0:T(8,128)S(1)} %all-to-all-done.2) | copy-start | bytes 4718596
  90.5 23.8 %all-to-all-start.3 = ((f32[16,192,128]{2,1,0:T(8,128)}), f32[16,192,128]{2,1,0:T(8,128)}, u32[]{:S(2)}, u32[]{:S(2)}) async-start(f32[16,192,128]{2,1,0:T(8,128)} %bitcast.8), calls=%async_computation.3 | async-start | bytes 3145728 | tf_op jit(solution)/shard_map/all_to_all | solution.py:83
  172.2 1.4 copy-start.4
  281.0 63.8 %copy-start.1 = (f32[2,1,128,256]{3,2,1,0:T(8,128)}, f32[2,1,128,256]{3,2,1,0:T(8,128)S(1)}, u32[]{:S(2)}) copy-start(f32[2,1,128,256]{3,2,1,0:T(8,128)S(1)} %get-tuple-element.31) | copy-start | bytes 786436
  356.8 1.4 copy-start.5
  399.4 65.3 %copy-start.2 = (f32[2,1,128,256]{3,2,1,0:T(8,128)S(1)}, f32[2,1,128,256]{3,2,1,0:T(8,128)}, u32[]{:S(2)}) copy-start(f32[2,1,128,256]{3,2,1,0:T(8,128)} %copy-done.1) | copy-start | bytes 786436
